TPU v7x, 256 devices: a whole 4x4x8 slice. The times are simulated.
256 devices in a mesh: frames: 32 (over z, x_lo, core), runs: 8 (over y, x_hi).
Axes of the slice: x: 4 (x_hi: 2, x_lo: 2; x = x_hi * 2 + x_lo), y: 4, z: 8, core: 2. Of those that a mesh axis runs over, the one named last changes fastest.
Arguments:
- inputs: bfloat16 [8, 131072, 256], P('runs', 'frames'), may hold values from -6 to 6
- first_layer_weight: bfloat16 [3, 256, 256], replicated, may hold values from -0.21875 to 0.21875
- first_layer_bias: bfloat16 [256], replicated, may hold values from -3 to 3
- second_layer_weight: bfloat16 [3, 256, 256], replicated, may hold values from -0.21875 to 0.21875
- second_layer_bias: bfloat16 [256], replicated, may hold values from -3 to 3
- upstream: bfloat16 [8, 131072, 256], P('runs', 'frames'), may hold values from -6 to 6
Outputs:
- outputs: bfloat16 [8, 131072, 256], P('runs', 'frames')
- grad_input: bfloat16 [8, 131072, 256], P('runs', 'frames')
- grad_w_first: float32 [3, 256, 256], replicated
- grad_b_first: float32 [256], replicated
- grad_w_second: float32 [3, 256, 256], replicated
- grad_b_second: float32 [256], replicated
All inputs are finite; a program needn't handle non-finite values.
Results may differ from a plain program's by a relative error of at most 0.007.
Values may be sent and summed in bfloat16 or wider, within the bound.
A program may use at most 128 MiB of HBM per device.

v0:
```python
import math
import jax
import jax.numpy as jnp
from jax import lax
from jax.sharding import PartitionSpec as P

FIRST_SPACING = 256
SECOND_SPACING = 512


def passed_along(block, axis, distance):
    devices = range(lax.axis_size(axis))
    route = [(i - distance, i) for i in devices if i - distance in devices]
    return lax.ppermute(block, axis, route)


def gelu_slope(pre, grad):
    return jax.vjp(jax.nn.gelu, pre)[1](grad)[0]


def causal_conv_apply(extended, weights, bias, dilation, frame_count):
    total = bias.astype(jnp.float32)[None, None, :]
    for k in range(3):
        start = 2 * dilation - k * dilation
        total = total + jnp.einsum(
            "rtc,cd->rtd",
            extended[:, start : start + frame_count],
            weights[k],
            preferred_element_type=jnp.float32,
        )
    return total


def causal_conv_weight_gradient(extended, grad, dilation, frame_count):
    pieces = []
    for k in range(3):
        start = 2 * dilation - k * dilation
        pieces.append(
            jnp.einsum(
                "rtc,rtd->cd",
                extended[:, start : start + frame_count],
                grad,
                preferred_element_type=jnp.float32,
            )
        )
    return jnp.stack(pieces)


def local_terms(grad, weights, dilation, frame_count):
    padded = jnp.pad(grad, ((0, 0), (0, 2 * dilation), (0, 0)))
    total = jnp.zeros(grad.shape, jnp.float32)
    for k in range(3):
        start = k * dilation
        total = total + jnp.einsum(
            "rtd,cd->rtc",
            padded[:, start : start + frame_count],
            weights[k],
            preferred_element_type=jnp.float32,
        )
    return total


def rim_terms(grad, weights, dilation):
    far_terms = jnp.einsum(
        "rtd,cd->rtc", grad[:, : 2 * dilation], weights[2], preferred_element_type=jnp.float32
    )
    near_terms = jnp.einsum(
        "rtd,cd->rtc", grad[:, :dilation], weights[1], preferred_element_type=jnp.float32
    )
    return far_terms + jnp.pad(near_terms, ((0, 0), (dilation, 0), (0, 0)))


def place_tail(arrived, frame_count, dilation):
    return jnp.pad(arrived, ((0, 0), (frame_count - 2 * dilation, 0), (0, 0)))


def causal_conv_input_gradient(grad, weights, dilation, frame_count, layer):
    total = local_terms(grad, weights, dilation, frame_count)
    rim_part = rim_terms(grad, weights, dilation)
    if layer == 2:
        arrived = passed_along(rim_part.astype(jnp.bfloat16), "frames", -1).astype(rim_part.dtype)
    else:
        arrived = passed_along(rim_part.astype(jnp.bfloat16), "frames", -1).astype(rim_part.dtype)
    return total + place_tail(arrived, frame_count, dilation)


def body(
    inputs, first_layer_weight, first_layer_bias, second_layer_weight, second_layer_bias, upstream
):
    frame_count = inputs.shape[1]
    prior_frames = passed_along(inputs[:, frame_count - 2 * FIRST_SPACING :], "frames", 1)
    input_with_history = jnp.concatenate([prior_frames, inputs], axis=1)
    first_preactivation = causal_conv_apply(
        input_with_history, first_layer_weight, first_layer_bias, FIRST_SPACING, frame_count
    )
    hidden_state = (inputs.astype(jnp.float32) + jax.nn.gelu(first_preactivation)).astype(
        jnp.bfloat16
    )
    prior_hidden_frames = passed_along(
        hidden_state[:, frame_count - 2 * SECOND_SPACING :], "frames", 1
    )
    hidden_with_history = jnp.concatenate([prior_hidden_frames, hidden_state], axis=1)
    second_preactivation = causal_conv_apply(
        hidden_with_history, second_layer_weight, second_layer_bias, SECOND_SPACING, frame_count
    )
    result = (hidden_state.astype(jnp.float32) + jax.nn.gelu(second_preactivation)).astype(
        jnp.bfloat16
    )
    output_gradient = upstream.astype(jnp.float32)
    second_layer_gradient = gelu_slope(second_preactivation, output_gradient).astype(jnp.bfloat16)
    second_weight_delta = causal_conv_weight_gradient(
        hidden_with_history, second_layer_gradient, SECOND_SPACING, frame_count
    )
    db_second = jnp.sum(second_layer_gradient.astype(jnp.float32), axis=(0, 1))
    hidden_gradient = output_gradient + causal_conv_input_gradient(
        second_layer_gradient, second_layer_weight, SECOND_SPACING, frame_count, 2
    )
    first_layer_gradient = gelu_slope(first_preactivation, hidden_gradient).astype(jnp.bfloat16)
    input_gradient_rows = (
        hidden_gradient
        + causal_conv_input_gradient(
            first_layer_gradient, first_layer_weight, FIRST_SPACING, frame_count, 1
        )
    ).astype(jnp.bfloat16)
    first_weight_delta = causal_conv_weight_gradient(
        input_with_history, first_layer_gradient, FIRST_SPACING, frame_count
    )
    db_first = jnp.sum(first_layer_gradient.astype(jnp.float32), axis=(0, 1))
    factor = 1.0 / math.sqrt(
        inputs.shape[0] * lax.axis_size("runs") * frame_count * lax.axis_size("frames")
    )
    sum_w_first, sum_b_first, sum_w_second, sum_b_second = lax.psum(
        (first_weight_delta, db_first, second_weight_delta, db_second), ("frames", "runs")
    )
    sum_w_first = sum_w_first * factor
    sum_b_first = sum_b_first * factor
    sum_w_second = sum_w_second * factor
    sum_b_second = sum_b_second * factor
    return (result, input_gradient_rows, sum_w_first, sum_b_first, sum_w_second, sum_b_second)


def solution(mesh):
    return jax.shard_map(
        body,
        mesh=mesh,
        in_specs=(P("runs", "frames", None), P(), P(), P(), P(), P("runs", "frames", None)),
        out_specs=(P("runs", "frames", None), P("runs", "frames", None), P(), P(), P(), P()),
        check_vma=False,
    )
```

profile of v0, /device:TPU:2, one launch (start us, length us, event | category | flops | bytes accessed | tf_op | source)
XLA Modules:
  0.0 347.0 jit_solution(14924929035905152933)
XLA Ops:
  7.2 0.0 all-reduce.10.cloned.1.call-start
  7.2 1.0 slice.77
  8.2 1.9 collective-permute-start
  10.1 0.7 convert_element_type.57
  10.8 2.5 convolution_add_fusion.9
  13.2 0.0 copy-start.1
  13.2 2.6 collective-permute-done
  15.9 0.1 constant_dynamic-update-slice_fusion
  16.1 0.7 convolution_add_fusion.8
  16.8 0.0 copy-start.4
  16.8 0.0 copy-start.3
  16.8 1.9 fusion.24
  18.8 2.1 collective-permute-start.1
  20.9 0.7 convolution_add_fusion.6
  21.6 0.0 copy-start.2
  21.6 7.7 %collective-permute-done.1 = bf16[1,1024,256]{2,1,0:T(8,128)(2,1)S(1)} collective-permute-done((bf16[1,1024,256]{2,1,0:T(8,128)(2,1)S(1)}, bf16[1,1024,256]{2,1,0:T(8,128)(2,1)S(1)}, u32[]{:S(2)}, u32[]{:S(2)}) %collective-permute-start.1) | collective-permute-done | bytes 524320 | tf_op jit(solution)/shard_map/ppermute | solution.py:14
  29.3 0.8 convolution_add_fusion.5
  30.1 0.0 copy-done.2
  30.1 7.2 %convert_reduce_fusion = (f32[256]{0:T(256)S(1)}, bf16[1,4096,256]{2,1,0:T(8,128)(2,1)S(1)}, bf16[1,4096,256]{2,1,0:T(8,128)(2,1)}) fusion(bf16[1,4096,256]{2,1,0:T(8,128)(2,1)S(1)} %copy-done.2, bf16[1,4096,256]{2,1,0:T(8,128)(2,1)S(1)} %get-tuple-element.21, f32[4096,256]{1,0:T(8,128)S(1)} %convolution_add_fusion.5, ...), kind=kOutput, calls=%fused_computation.47 | convolution fusion | flops 570425088 | bytes 15336448 | tf_op jit(solution)/shard_map/rtc,cd->rtd/dot_general | solution.py:25
  37.3 1.0 fusion.62
  38.3 0.2 convolution_bitcast_fusion.2
  38.5 0.7 fusion.52
  39.3 0.3 fusion.59
  39.6 2.1 collective-permute-start.2
  41.7 1.0 fusion.67
  42.7 1.0 fusion.70
  43.6 0.9 pad_maximum_fusion.2
  44.6 0.8 convolution_add_fusion.3
  45.3 2.9 collective-permute-done.2
  48.2 6.9 %convert_reduce_fusion.1 = (f32[256]{0:T(256)S(1)}, bf16[1,4096,256]{2,1,0:T(8,128)(2,1)S(1)}, f32[1,4096,256]{2,1,0:T(8,128)}) fusion(f32[4096,256]{1,0:T(8,128)S(1)} %get-tuple-element.22, bf16[1,1024,256]{2,1,0:T(8,128)(2,1)S(1)} %collective-permute-done.2, bf16[1,4096,256]{2,1,0:T(8,128)(2,1)S(1)} %copy-done.2, ...), kind=kOutput, calls=%fused_computation.48 | convolution fusion | flops 565182208 | bytes 19530752 | tf_op jit(solution)/shard_map/rtd,cd->rtc/dot_general | solution.py:54
  55.1 1.0 fusion.78
  56.1 1.0 fusion.81
  57.1 0.8 fusion.73
  57.9 0.2 convolution_bitcast_fusion.3
  58.1 0.7 fusion.44
  58.8 0.3 fusion.61
  59.1 3.8 %collective-permute-start.3 = (bf16[1,512,256]{2,1,0:T(8,128)(2,1)S(1)}, bf16[1,512,256]{2,1,0:T(8,128)(2,1)S(1)}, u32[]{:S(2)}, u32[]{:S(2)}) collective-permute-start(bf16[1,512,256]{2,1,0:T(8,128)(2,1)S(1)} %fusion.61), channel_id=1, source_target_pairs={{8,0},{16,8},{24,16},{32,24},{40,32},{48,40},{56,48},{64,56},{72,6... | collective-permute-start | bytes 786440 | tf_op jit(solution)/shard_map/ppermute | solution.py:14
  62.9 2.8 convolution_add_fusion.1
  65.7 0.9 pad_maximum_fusion.1
  66.6 0.0 all-reduce.10.cloned.1.call-update
  66.6 82.8 %all-reduce.6 = (f32[256]{0:T(256)S(1)}, f32[256]{0:T(256)S(1)}) all-reduce(f32[256]{0:T(256)S(1)} %get-tuple-element.18, f32[256]{0:T(256)S(1)} %get-tuple-element.16), channel_id=1, replica_groups=mesh['frames'=32,'runs'=8] {'frames','runs'}, use_global_device_ids=true, to_apply=%region_2.3 | all-reduce | flops 512 | bytes 4096 | tf_op jit(solution)/shard_map/psum | solution.py:132
  149.4 0.6 broadcast_multiply_fusion.2
  150.0 0.0 collective-permute-done.3
  150.0 8.1 %add_convert_fusion = bf16[1,4096,256]{2,1,0:T(8,128)(2,1)} fusion(f32[4096,256]{1,0:T(8,128)} %convolution_add_fusion.1, bf16[1,4096,256]{2,1,0:T(8,128)(2,1)S(1)} %get-tuple-element.19, bf16[1,512,256]{2,1,0:T(8,128)(2,1)S(1)} %collective-permute-done.3, f32[1,4096,256]{2,1,0:T(8,128)} %get-tuple-element.23, ...), kind=kOutput, calls=%fused_computation.49 | convolution fusion | flops 546308096 | bytes 15597568 | tf_op jit(solution)/shard_map/rtd,cd->rtc/dot_general | solution.py:54
  158.1 178.3 %all-reduce.10.cloned.1.call-done = (f32[3,256,256]{1,2,0:T(8,128)}, f32[3,256,256]{1,2,0:T(8,128)}) async-done(((f32[3,256,256]{1,2,0:T(8,128)}, f32[3,256,256]{1,2,0:T(8,128)}), (f32[3,256,256]{1,2,0:T(8,128)}, f32[3,256,256]{1,2,0:T(8,128)})) %all-reduce.10.cloned.1.call-update) | async-done | bytes 1572880 | tf_op jit(solution)/shard_map/psum | solution.py:132
  336.4 1.5 broadcast_multiply_fusion
  337.8 1.1 copy.18
  339.0 1.1 copy.17
  (8 shorter events, 0.1 us)
Async XLA Ops:
  7.2 329.2 %all-reduce.10.cloned.1.call-start = ((), (), s32[]{:S(2)}) async-start(), calls=%async_computation | async-start | bytes 3145728 | tf_op jit(solution)/shard_map/psum | solution.py:132
  8.2 7.7 %collective-permute-start = (bf16[1,512,256]{2,1,0:T(8,128)(2,1)S(1)}, bf16[1,512,256]{2,1,0:T(8,128)(2,1)S(1)}, u32[]{:S(2)}, u32[]{:S(2)}) collective-permute-start(bf16[1,512,256]{2,1,0:T(8,128)(2,1)S(1)} %slice.77), channel_id=1, source_target_pairs={{0,8},{8,16},{16,24},{24,32},{32,40},{40,48},{48,56},{56,64},{64,7... | collective-permute-start | bytes 786440 | tf_op jit(solution)/shard_map/ppermute | solution.py:14
  10.8 5.1 %copy-start = (bf16[1,4096,256]{2,1,0:T(8,128)(2,1)S(1)}, bf16[1,4096,256]{2,1,0:T(8,128)(2,1)}, u32[]{:S(2)}) copy-start(bf16[1,4096,256]{2,1,0:T(8,128)(2,1)} %param.6) | copy-start | bytes 6291460
  13.2 2.8 copy-start.1
  16.8 4.1 %copy-start.4 = (bf16[256]{0:T(256)(128)(2,1)S(1)}, bf16[256]{0:T(256)(128)(2,1)}, u32[]{:S(2)}) copy-start(bf16[256]{0:T(256)(128)(2,1)} %param.10) | copy-start | bytes 1540
  16.8 4.1 %copy-start.3 = (bf16[3,256,256]{2,1,0:T(8,128)(2,1)S(1)}, bf16[3,256,256]{2,1,0:T(8,128)(2,1)}, u32[]{:S(2)}) copy-start(bf16[3,256,256]{2,1,0:T(8,128)(2,1)} %param.9) | copy-start | bytes 1179652
  18.8 10.5 %collective-permute-start.1 = (bf16[1,1024,256]{2,1,0:T(8,128)(2,1)S(1)}, bf16[1,1024,256]{2,1,0:T(8,128)(2,1)S(1)}, u32[]{:S(2)}, u32[]{:S(2)}) collective-permute-start(bf16[1,1024,256]{2,1,0:T(8,128)(2,1)S(1)} %slice.98), channel_id=1, source_target_pairs={{0,8},{8,16},{16,24},{24,32},{32,40},{40,48},{48,56},{56,64},{64,7... | collective-permute-start | bytes 1572872 | tf_op jit(solution)/shard_map/ppermute | solution.py:14
  21.6 8.4 %copy-start.2 = (bf16[1,4096,256]{2,1,0:T(8,128)(2,1)S(1)}, bf16[1,4096,256]{2,1,0:T(8,128)(2,1)}, u32[]{:S(2)}) copy-start(bf16[1,4096,256]{2,1,0:T(8,128)(2,1)} %param.11) | copy-start | bytes 6291460
  39.6 8.6 %collective-permute-start.2 = (bf16[1,1024,256]{2,1,0:T(8,128)(2,1)S(1)}, bf16[1,1024,256]{2,1,0:T(8,128)(2,1)S(1)}, u32[]{:S(2)}, u32[]{:S(2)}) collective-permute-start(bf16[1,1024,256]{2,1,0:T(8,128)(2,1)S(1)} %fusion.59), channel_id=1, source_target_pairs={{8,0},{16,8},{24,16},{32,24},{40,32},{48,40},{56,48},{64,56},{72,6... | collective-permute-start | bytes 1572872 | tf_op jit(solution)/shard_map/ppermute | solution.py:14
  59.1 90.9 %collective-permute-start.3 = (bf16[1,512,256]{2,1,0:T(8,128)(2,1)S(1)}, bf16[1,512,256]{2,1,0:T(8,128)(2,1)S(1)}, u32[]{:S(2)}, u32[]{:S(2)}) collective-permute-start(bf16[1,512,256]{2,1,0:T(8,128)(2,1)S(1)} %fusion.61), channel_id=1, source_target_pairs={{8,0},{16,8},{24,16},{32,24},{40,32},{48,40},{56,48},{64,56},{72,6... | collective-permute-start | bytes 786440 | tf_op jit(solution)/shard_map/ppermute | solution.py:14
Sparse Core Ops, SparseCore 0:
  66.7 269.5 all-reduce.9
where the time goes:
time: 347 us
  waiting for transfers between devices  191 us (55%)
  blocking collectives  82.8 us (24%)
  matrix products  40.5 us (12%)
  between operations  14.3 us (4%)
  starting transfers between devices  9.95 us (3%)
  other arithmetic  4.58 us (1%)
  local copies, waits for them, and re-layouts  3.49 us (1%)
    psum x1, waiting for transfers between devices, body(): lax.psum((first_weight_delta, db_first, second_weight_delta, db_second),...  178 us
    psum x1, blocking collectives, body(): lax.psum((first_weight_delta, db_first, second_weight_delta, db_second),...  82.8 us
    dot_general x6, matrix products, local_terms(): jnp.einsum('rtd,cd->rtc', padded[:, start:start + frame_count], weights[k...  20 us
    dot_general x6, matrix products, causal_conv_apply(): jnp.einsum('rtc,cd->rtd', extended[:, start:start + frame_count], weights...  13.8 us
    ppermute x4, waiting for transfers between devices, passed_along(): return lax.ppermute(block, axis, route)  13.1 us
    ppermute x4, starting transfers between devices, passed_along(): return lax.ppermute(block, axis, route)  9.91 us
  transfers between devices with their start and end apart: 5, of which 4 were waited for; matrix products, arithmetic and copies ran while one was open for 6% of the time, Pallas kernels for 0%

commit v1 on v0

--- a/solution.py
+++ b/solution.py
@@ -130,7 +130,7 @@
         inputs.shape[0] * lax.axis_size("runs") * frame_count * lax.axis_size("frames")
     )
     sum_w_first, sum_b_first, sum_w_second, sum_b_second = lax.psum(
-        (first_weight_delta, db_first, second_weight_delta, db_second), ("frames", "runs")
+        lax.psum((first_weight_delta, db_first, second_weight_delta, db_second), "runs"), "frames"
     )
     sum_w_first = sum_w_first * factor
     sum_b_first = sum_b_first * factor

time: 347 us -> 412 us (1.19); the launches traced: 347 us -> 407 us
  waiting for transfers between devices: 191 us -> 262 us
  blocking collectives: 82.8 us -> 72.2 us
    psum x0 -> x1, waiting for transfers between devices: none -> 144 us  [body(): lax.psum(lax.psum((first_weight_delta, db_first, second_weight_delta, db_...]
    psum x1, waiting for transfers between devices: 178 us -> 104 us  [body(): lax.psum((first_weight_delta, db_first, second_weight_delta, db_second),...]
    psum x1, blocking collectives: 82.8 us -> 22.1 us  [body(): lax.psum((first_weight_delta, db_first, second_weight_delta, db_second),...]
    psum x0 -> x1, blocking collectives: none -> 50.1 us  [body(): lax.psum(lax.psum((first_weight_delta, db_first, second_weight_delta, db_...]
  transfers between devices with their start and end apart: 5 -> 6, of which waited for: 4 -> 5; matrix products, arithmetic and copies ran while one was open for 6% -> 5% of each run, Pallas kernels for 0% -> 0%
where the time goes in v1:
time: 412 us; the launch traced here: 407 us
  waiting for transfers between devices  262 us (64%)
  blocking collectives  72.2 us (18%)
  matrix products  40.5 us (10%)
  between operations  14.3 us (3%)
  starting transfers between devices  9.99 us (2%)
  other arithmetic  4.63 us (1%)
    psum x1, waiting for transfers between devices, body(): lax.psum(lax.psum((first_weight_delta, db_first, second_weight_delta, db_...  144 us
    psum x1, waiting for transfers between devices, body(): lax.psum((first_weight_delta, db_first, second_weight_delta, db_second),...  104 us
    psum x1, blocking collectives, body(): lax.psum(lax.psum((first_weight_delta, db_first, second_weight_delta, db_...  50.1 us
    psum x1, blocking collectives, body(): lax.psum((first_weight_delta, db_first, second_weight_delta, db_second),...  22.1 us
    dot_general x6, matrix products, local_terms(): jnp.einsum('rtd,cd->rtc', padded[:, start:start + frame_count], weights[k...  20 us
    dot_general x6, matrix products, causal_conv_apply(): jnp.einsum('rtc,cd->rtd', extended[:, start:start + frame_count], weights...  13.8 us
    ppermute x4, waiting for transfers between devices, passed_along(): return lax.ppermute(block, axis, route)  13.2 us
    ppermute x4, starting transfers between devices, passed_along(): return lax.ppermute(block, axis, route)  9.91 us
  transfers between devices with their start and end apart: 6, of which 5 were waited for; matrix products, arithmetic and copies ran while one was open for 5% of the time, Pallas kernels for 0%

profile of v1, /device:TPU:2, one launch (start us, length us, event | category | flops | bytes accessed | tf_op | source)
XLA Modules:
  0.0 406.9 jit_solution(17970216004452377093)
XLA Ops:
  7.2 0.0 all-reduce.15.cloned.1.call-start
  7.2 1.0 slice.77
  8.2 1.9 collective-permute-start
  10.1 0.7 convert_element_type.57
  10.8 2.5 convolution_add_fusion.9
  13.2 0.0 copy-start.1
  13.2 2.6 collective-permute-done
  15.9 0.1 constant_dynamic-update-slice_fusion
  16.1 0.7 convolution_add_fusion.8
  16.8 0.0 copy-start.3
  16.8 2.0 fusion.24
  18.8 2.1 collective-permute-start.1
  20.9 0.7 convolution_add_fusion.6
  21.7 7.7 %collective-permute-done.1 = bf16[1,1024,256]{2,1,0:T(8,128)(2,1)S(1)} collective-permute-done((bf16[1,1024,256]{2,1,0:T(8,128)(2,1)S(1)}, bf16[1,1024,256]{2,1,0:T(8,128)(2,1)S(1)}, u32[]{:S(2)}, u32[]{:S(2)}) %collective-permute-start.1) | collective-permute-done | bytes 524320 | tf_op jit(solution)/shard_map/ppermute | solution.py:14
  29.3 0.8 convolution_add_fusion.5
  30.1 7.2 %convert_reduce_fusion = (f32[256]{0:T(256)S(1)}, bf16[1,4096,256]{2,1,0:T(8,128)(2,1)S(1)}, bf16[1,4096,256]{2,1,0:T(8,128)(2,1)}) fusion(bf16[1,4096,256]{2,1,0:T(8,128)(2,1)S(1)} %copy-done.2, bf16[1,4096,256]{2,1,0:T(8,128)(2,1)S(1)} %get-tuple-element.25, f32[4096,256]{1,0:T(8,128)S(1)} %convolution_add_fusion.5, ...), kind=kOutput, calls=%fused_computation.47 | convolution fusion | flops 570425088 | bytes 15336448 | tf_op jit(solution)/shard_map/rtc,cd->rtd/dot_general | solution.py:25
  37.3 1.0 fusion.62
  38.3 0.2 convolution_bitcast_fusion.2
  38.5 0.7 fusion.52
  39.3 0.3 fusion.59
  39.6 2.1 collective-permute-start.2
  41.7 1.0 fusion.67
  42.7 1.0 fusion.70
  43.7 0.9 pad_maximum_fusion.2
  44.6 0.8 convolution_add_fusion.3
  45.4 2.9 collective-permute-done.2
  48.2 6.9 %convert_reduce_fusion.1 = (f32[256]{0:T(256)S(1)}, bf16[1,4096,256]{2,1,0:T(8,128)(2,1)S(1)}, f32[1,4096,256]{2,1,0:T(8,128)}) fusion(f32[4096,256]{1,0:T(8,128)S(1)} %get-tuple-element.26, bf16[1,1024,256]{2,1,0:T(8,128)(2,1)S(1)} %collective-permute-done.2, bf16[1,4096,256]{2,1,0:T(8,128)(2,1)S(1)} %copy-done.2, ...), kind=kOutput, calls=%fused_computation.48 | convolution fusion | flops 565182208 | bytes 19530752 | tf_op jit(solution)/shard_map/rtd,cd->rtc/dot_general | solution.py:54
  55.1 1.0 fusion.78
  56.1 1.0 fusion.81
  57.1 0.8 fusion.73
  57.9 0.9 pad_maximum_fusion.1
  58.8 0.0 all-reduce.15.cloned.1.call-update
  58.8 0.0 all-reduce.13.cloned.1.call-start
  58.9 0.2 convolution_bitcast_fusion.3
  59.1 0.3 fusion.61
  59.4 3.8 collective-permute-start.3
  63.2 104.5 %all-reduce.15.cloned.1.call-done = (f32[3,256,256]{1,2,0:T(8,128)}, f32[3,256,256]{1,2,0:T(8,128)}) async-done(((f32[3,256,256]{1,2,0:T(8,128)}, f32[3,256,256]{1,2,0:T(8,128)}), (f32[3,256,256]{1,2,0:T(8,128)}, f32[3,256,256]{1,2,0:T(8,128)})) %all-reduce.15.cloned.1.call-update) | async-done | bytes 1572880 | tf_op jit(solution)/shard_map/psum | solution.py:133
  167.7 0.0 all-reduce.13.cloned.1.call-update
  167.7 0.7 fusion.44
  168.4 2.8 convolution_add_fusion.1
  171.2 22.1 %all-reduce.8 = (f32[256]{0:T(256)S(1)}, f32[256]{0:T(256)S(1)}) all-reduce(f32[256]{0:T(256)S(1)} %get-tuple-element.22, f32[256]{0:T(256)S(1)} %get-tuple-element.20), channel_id=1, replica_groups=mesh['frames'=32,'runs'=8] {'runs'}, use_global_device_ids=true, to_apply=%region_3.4 | all-reduce | flops 512 | bytes 4096 | tf_op jit(solution)/shard_map/psum | solution.py:133
  193.3 50.1 %all-reduce.6 = (f32[256]{0:T(256)S(1)}, f32[256]{0:T(256)S(1)}) all-reduce(f32[256]{0:T(256)S(1)} %get-tuple-element.16, f32[256]{0:T(256)S(1)} %get-tuple-element.17), channel_id=1, replica_groups=mesh['frames'=32,'runs'=8] {'frames'}, use_global_device_ids=true, to_apply=%region_4.5 | all-reduce | flops 512 | bytes 4096 | tf_op jit(solution)/shard_map/psum | solution.py:132
  243.4 0.6 broadcast_multiply_fusion.2
  244.0 8.1 %add_convert_fusion = bf16[1,4096,256]{2,1,0:T(8,128)(2,1)} fusion(f32[4096,256]{1,0:T(8,128)} %convolution_add_fusion.1, bf16[1,4096,256]{2,1,0:T(8,128)(2,1)S(1)} %get-tuple-element.23, bf16[1,512,256]{2,1,0:T(8,128)(2,1)S(1)} %collective-permute-done.3, f32[1,4096,256]{2,1,0:T(8,128)} %get-tuple-element.27, ...), kind=kOutput, calls=%fused_computation.49 | convolution fusion | flops 546308096 | bytes 15597568 | tf_op jit(solution)/shard_map/rtd,cd->rtc/dot_general | solution.py:54
  252.1 144.2 %all-reduce.13.cloned.1.call-done = (f32[3,256,256]{1,2,0:T(8,128)}, f32[3,256,256]{1,2,0:T(8,128)}) async-done(((f32[3,256,256]{1,2,0:T(8,128)}, f32[3,256,256]{1,2,0:T(8,128)}), (f32[3,256,256]{1,2,0:T(8,128)}, f32[3,256,256]{1,2,0:T(8,128)})) %all-reduce.13.cloned.1.call-update) | async-done | bytes 1572880 | tf_op jit(solution)/shard_map/psum | solution.py:132
  396.3 1.5 broadcast_multiply_fusion
  397.8 1.2 copy.18
  398.9 1.1 copy.17
  (12 shorter events, 0.1 us)
Async XLA Ops:
  7.2 160.5 %all-reduce.15.cloned.1.call-start = ((), (), s32[]{:S(2)}) async-start(), calls=%async_computation.1 | async-start | bytes 3145728 | tf_op jit(solution)/shard_map/psum | solution.py:133
  8.2 7.7 %collective-permute-start = (bf16[1,512,256]{2,1,0:T(8,128)(2,1)S(1)}, bf16[1,512,256]{2,1,0:T(8,128)(2,1)S(1)}, u32[]{:S(2)}, u32[]{:S(2)}) collective-permute-start(bf16[1,512,256]{2,1,0:T(8,128)(2,1)S(1)} %slice.77), channel_id=1, source_target_pairs={{0,8},{8,16},{16,24},{24,32},{32,40},{40,48},{48,56},{56,64},{64,7... | collective-permute-start | bytes 786440 | tf_op jit(solution)/shard_map/ppermute | solution.py:14
  10.8 5.1 %copy-start = (bf16[1,4096,256]{2,1,0:T(8,128)(2,1)S(1)}, bf16[1,4096,256]{2,1,0:T(8,128)(2,1)}, u32[]{:S(2)}) copy-start(bf16[1,4096,256]{2,1,0:T(8,128)(2,1)} %param.6) | copy-start | bytes 6291460
  13.2 2.8 copy-start.1
  16.8 4.1 %copy-start.4 = (bf16[256]{0:T(256)(128)(2,1)S(1)}, bf16[256]{0:T(256)(128)(2,1)}, u32[]{:S(2)}) copy-start(bf16[256]{0:T(256)(128)(2,1)} %param.10) | copy-start | bytes 1540
  16.8 4.1 %copy-start.3 = (bf16[3,256,256]{2,1,0:T(8,128)(2,1)S(1)}, bf16[3,256,256]{2,1,0:T(8,128)(2,1)}, u32[]{:S(2)}) copy-start(bf16[3,256,256]{2,1,0:T(8,128)(2,1)} %param.9) | copy-start | bytes 1179652
  18.8 10.5 %collective-permute-start.1 = (bf16[1,1024,256]{2,1,0:T(8,128)(2,1)S(1)}, bf16[1,1024,256]{2,1,0:T(8,128)(2,1)S(1)}, u32[]{:S(2)}, u32[]{:S(2)}) collective-permute-start(bf16[1,1024,256]{2,1,0:T(8,128)(2,1)S(1)} %slice.98), channel_id=1, source_target_pairs={{0,8},{8,16},{16,24},{24,32},{32,40},{40,48},{48,56},{56,64},{64,7... | collective-permute-start | bytes 1572872 | tf_op jit(solution)/shard_map/ppermute | solution.py:14
  21.6 8.5 %copy-start.2 = (bf16[1,4096,256]{2,1,0:T(8,128)(2,1)S(1)}, bf16[1,4096,256]{2,1,0:T(8,128)(2,1)}, u32[]{:S(2)}) copy-start(bf16[1,4096,256]{2,1,0:T(8,128)(2,1)} %param.11) | copy-start | bytes 6291460
  39.6 8.6 %collective-permute-start.2 = (bf16[1,1024,256]{2,1,0:T(8,128)(2,1)S(1)}, bf16[1,1024,256]{2,1,0:T(8,128)(2,1)S(1)}, u32[]{:S(2)}, u32[]{:S(2)}) collective-permute-start(bf16[1,1024,256]{2,1,0:T(8,128)(2,1)S(1)} %fusion.59), channel_id=1, source_target_pairs={{8,0},{16,8},{24,16},{32,24},{40,32},{48,40},{56,48},{64,56},{72,6... | collective-permute-start | bytes 1572872 | tf_op jit(solution)/shard_map/ppermute | solution.py:14
  58.8 337.4 %all-reduce.13.cloned.1.call-start = ((), (), s32[]{:S(2)}) async-start(), calls=%async_computation | async-start | bytes 3145728 | tf_op jit(solution)/shard_map/psum | solution.py:132
  59.4 184.6 %collective-permute-start.3 = (bf16[1,512,256]{2,1,0:T(8,128)(2,1)S(1)}, bf16[1,512,256]{2,1,0:T(8,128)(2,1)S(1)}, u32[]{:S(2)}, u32[]{:S(2)}) collective-permute-start(bf16[1,512,256]{2,1,0:T(8,128)(2,1)S(1)} %fusion.61), channel_id=1, source_target_pairs={{8,0},{16,8},{24,16},{32,24},{40,32},{48,40},{56,48},{64,56},{72,6... | collective-permute-start | bytes 786440 | tf_op jit(solution)/shard_map/ppermute | solution.py:14
Sparse Core Ops, SparseCore 0:
  59.0 108.6 all-reduce.14
  170.3 225.8 all-reduce.12
